TPU v7x, 128 devices: a whole 4x4x4 slice. The times are simulated.
128 devices in a mesh: slab: 16 (over z, x), pencil: 8 (over y, core).
Axes of the slice: x: 4, y: 4, z: 4, core: 2. Of those that a mesh axis runs over, the one named last changes fastest.
Arguments:
- a_blocks: float32 [256, 64, 20480], P('slab', 'pencil'), may hold values from -1 to 8, as said below
- col_codes: int32 [256, 64, 5], P('slab', 'pencil'), may hold values from 0 to 8, as said below
- agg_of: int32 [256, 64], P('slab', 'pencil'), may hold values from 0 to 2047, as said below
- test_vectors: float32 [256, 64, 2048], P('slab', 'pencil'), may hold values from -36 to 36
Outputs:
- relaxed: float32 [256, 64, 2048], P('slab', 'pencil')
- tiles: float32 [256, 64, 512], P('slab', 'pencil')
- products: float32 [256, 64, 2560], P('slab', 'pencil')
Inputs may be any that keep to these rules, and one draw needn't show every extreme that they name: `col_codes`: slot 0 of every block row is code 4, the block row itself; slots 1 to 4 hold different codes among the other eight of the 3 x 3 neighbourhood. `agg_of`: aggregate g is owned by device g // 16, devices numbered slab-major. On each device the block rows, in row-major order, form 64 groups of 2 consecutive block rows; all block rows of a group belong to aggregates of one owner, and the groups of one device go to different owners. Some owners receive a group from every device. `a_blocks`: the diagonal entries of every slot-0 block lie in [1.99, 8].
All inputs are finite; a program needn't handle non-finite values.
Results may differ from a plain program's by a relative error of at most 0.0003.
Values sent between devices are 32-bit elements; how exact they have to be, the bound alone decides.
A program may use at most 320 MiB of HBM per device.

v0:
```python
import math
import jax
import jax.numpy as jnp
from jax import lax
from jax.sharding import PartitionSpec as P

BLK = 64
NV = 32
NC = 8
KS = 5
ITERS = 2
OMEGA = 2.0 / 3.0
FULL_PRECISION = lax.Precision.HIGHEST


def with_halo(cells, sides, width):
    for axis, dim in sides:
        count = lax.axis_size(axis)
        ends = count - 1
        head = lax.slice_in_dim(cells, 0, width, axis=dim)
        tail = lax.slice_in_dim(cells, cells.shape[dim] - width, cells.shape[dim], axis=dim)
        cells = jnp.concatenate(
            [
                lax.ppermute(tail, axis, [(i, (i + 1) % count) for i in range(ends)]),
                cells,
                lax.ppermute(head, axis, [((i + 1) % count, i) for i in range(ends)]),
            ],
            axis=dim,
        )
    return cells


def coarse_modes(cells, coarse):
    centre = jnp.arange(cells, dtype=jnp.float32) + 0.5
    order = jnp.arange(coarse, dtype=jnp.float32)
    return jnp.cos(math.pi * centre[:, None] * order[None, :] / cells)


def solve_maps(coarse):
    gram = jnp.einsum("gkv,glv->gkl", coarse, coarse, precision=FULL_PRECISION)
    trace_sum = jnp.trace(gram, axis1=1, axis2=2)
    ridge = 0.1 * trace_sum / NC + 1e-06
    gram = gram + ridge[:, None, None] * jnp.eye(NC, dtype=jnp.float32)[None]
    lower = jnp.linalg.cholesky(gram)
    half_solved = jax.scipy.linalg.solve_triangular(lower, coarse, lower=True)
    solved = jax.scipy.linalg.solve_triangular(lower, half_solved, lower=True, trans=1)
    return jnp.swapaxes(solved, 1, 2)


def slot_index(col_codes):
    height, across_devices = (col_codes.shape[0], col_codes.shape[1])
    row_pos = jnp.arange(height, dtype=jnp.int32)[:, None, None] + col_codes // 3
    col_pos = jnp.arange(across_devices, dtype=jnp.int32)[None, :, None] + col_codes % 3
    return (row_pos * (across_devices + 2) + col_pos).reshape(-1)


def pick_rows(padded, flat_index, height, across_devices):
    features = padded.shape[2]
    flat = padded.reshape(padded.shape[0] * padded.shape[1], features)
    picked = jnp.take(flat, flat_index, axis=0)
    return picked.reshape(height, across_devices, KS, features)


def fit_slots(slot_coefficient, slot_ids, per_owner):
    members = (slot_ids[None, :] == jnp.arange(per_owner, dtype=jnp.int32)[:, None]).astype(
        jnp.float32
    )
    counts = jnp.sum(members, axis=1)
    summed = jnp.dot(
        members,
        slot_coefficient.reshape(slot_coefficient.shape[0], NC * NV),
        precision=FULL_PRECISION,
    )
    coarse = summed.reshape(per_owner, NC, NV) / jnp.maximum(counts, 1.0)[:, None, None]
    maps = solve_maps(coarse)
    return jnp.dot(members.T, maps.reshape(per_owner, NV * NC), precision=FULL_PRECISION)


def pack_slots(chosen_f, payload, group_list, capacity):
    flat = payload.reshape(group_list, capacity * payload.shape[1])
    packed = jnp.dot(chosen_f, flat, precision=FULL_PRECISION)
    return packed.reshape(chosen_f.shape[0], capacity, payload.shape[1])


def unpack_slots(chosen_f, received, block_rows):
    flat = received.reshape(received.shape[0], received.shape[1] * received.shape[2])
    return jnp.dot(chosen_f.T, flat, precision=FULL_PRECISION).reshape(
        block_rows, received.shape[2]
    )


def send_owner(payload, slot_ids):
    arrived, arrived_ids = (
        lax.all_to_all(payload, ("slab", "pencil"), split_axis=0, concat_axis=0, tiled=True),
        lax.all_to_all(slot_ids, ("slab", "pencil"), split_axis=0, concat_axis=0, tiled=True),
    )
    return (arrived, arrived_ids)


def send_back(payload):
    returned = lax.all_to_all(payload, ("slab", "pencil"), split_axis=0, concat_axis=0, tiled=True)
    return returned


def shards(a_blocks, col_codes, agg_of, test_vectors):
    height, across_devices = (agg_of.shape[0], agg_of.shape[1])
    n_slab = lax.axis_size("slab")
    n_pencil = lax.axis_size("pencil")
    devices = n_slab * n_pencil
    blocks = a_blocks.reshape(height, across_devices, KS, BLK, BLK)
    diagonal = jnp.diagonal(blocks[:, :, 0], axis1=-2, axis2=-1)
    block_wide = jnp.transpose(blocks, (0, 1, 3, 2, 4)).reshape(
        height, across_devices, BLK, KS * BLK
    )
    flat_index = slot_index(col_codes)
    candidate_vectors = test_vectors.reshape(height, across_devices, BLK, NV)
    for sweep in range(ITERS):
        padded = with_halo(
            candidate_vectors.reshape(height, across_devices, BLK * NV),
            (("slab", 0), ("pencil", 1)),
            1,
        )
        picked = pick_rows(padded, flat_index, height, across_devices).reshape(
            height, across_devices, KS * BLK, NV
        )
        image = jnp.einsum("ijor,ijrw->ijow", block_wide, picked, precision=FULL_PRECISION)
        candidate_vectors = candidate_vectors - OMEGA * image / diagonal[:, :, :, None]
    squares = jnp.sum(candidate_vectors * candidate_vectors, axis=(0, 1, 2))
    totals = lax.psum(squares, ("slab", "pencil"))
    scale = jnp.sqrt(totals / (height * across_devices * BLK * devices) + 1e-06)
    relaxed = candidate_vectors / scale
    block_rows = height * across_devices
    capacity = 2 * block_rows // devices
    group_list = devices // 2
    per_owner = block_rows // 8
    near_null_modes = coarse_modes(BLK, NC)
    row_vectors = relaxed.reshape(block_rows, BLK, NV)
    group_agg = agg_of.reshape(group_list, capacity)
    group_owner = group_agg[:, 0] // per_owner
    chosen = group_owner[None, :] == jnp.arange(devices, dtype=jnp.int32)[:, None]
    chosen_f = chosen.astype(jnp.float32)
    slot_ids = (
        jnp.sum(jnp.where(chosen[:, :, None], group_agg[None] % per_owner + 1, 0), axis=1) - 1
    )
    slot_count = devices * capacity
    outgoing = pack_slots(chosen_f, row_vectors.reshape(block_rows, BLK * NV), group_list, capacity)
    arrived, arrived_ids = send_owner(outgoing, slot_ids)
    slot_vector_rows = arrived.reshape(slot_count, BLK, NV)
    slot_coefficient = jnp.einsum(
        "wd,xwf->xdf", near_null_modes, slot_vector_rows, precision=FULL_PRECISION
    )
    slot_maps = fit_slots(slot_coefficient, arrived_ids.reshape(slot_count), per_owner)
    slot_tiles = jnp.einsum(
        "scv,svk->sck",
        slot_vector_rows,
        slot_maps.reshape(slot_count, NV, NC),
        precision=FULL_PRECISION,
    )
    returned = send_back(slot_tiles.reshape(devices, capacity, BLK * NC))
    tile_rows = unpack_slots(chosen_f, returned, block_rows).reshape(block_rows, BLK, NC)
    tile_grid = tile_rows.reshape(height, across_devices, BLK * NC)
    padded_tiles = with_halo(tile_grid, (("slab", 0), ("pencil", 1)), 1)
    picked_tiles = pick_rows(padded_tiles, flat_index, height, across_devices).reshape(
        height, across_devices, KS, BLK, NC
    )
    products = jnp.einsum("ijkoc,ijkcw->ijkow", blocks, picked_tiles, precision=FULL_PRECISION)
    return (
        relaxed.reshape(height, across_devices, BLK * NV),
        tile_grid,
        products.reshape(height, across_devices, KS * BLK * NC),
    )


def solution(mesh):
    in_specs = (
        P("slab", "pencil", None),
        P("slab", "pencil", None),
        P("slab", "pencil"),
        P("slab", "pencil", None),
    )
    out_specs = (P("slab", "pencil", None), P("slab", "pencil", None), P("slab", "pencil", None))
    return jax.shard_map(shards, mesh=mesh, in_specs=in_specs, out_specs=out_specs, check_vma=False)
```

profile of v0, /device:TPU:7, one launch (start us, length us, event | category | flops | bytes accessed | tf_op | source)
XLA Modules:
  0.0 639.7 jit_solution(15918062208513373529)
XLA Ops:
  0.6 0.9 fusion.53
  1.6 2.5 collective-permute-start.1
  4.1 4.9 collective-permute-start
  9.1 0.8 copy.189
  10.1 1.4 compare_and_fusion
  11.9 38.9 %copy.177 = f32[16,8,20480]{0,1,2:T(8,128)} copy(f32[16,8,20480]{2,1,0:T(8,128)} %param.6) | data formatting | bytes 20971520 | tf_op args[0]
  50.9 11.6 %slice_bitcast_fusion = f32[16,8,64,64]{0,1,3,2:T(8,128)} fusion(f32[16,8,5,64,64]{0,1,4,3,2:T(8,128)} %bitcast), kind=kLoop, calls=%fused_computation.6 | loop fusion | bytes 4194304 | tf_op jit(solution)/shard_map/squeeze | solution.py:111
  62.5 0.6 copy.175
  63.2 4.3 collective-permute-start.2
  67.6 1.9 collective-permute-start.3
  69.5 2.7 reshape.237
  72.2 3.8 copy.182
  76.0 6.4 %gather_fusion = f32[64,16,8]{1,2,0:T(8,128)S(1)} fusion(f32[16,8,64,64]{0,1,3,2:T(8,128)} %slice_bitcast_fusion, s32[64]{0:T(128)S(1)} %or_bitcast_fusion), kind=kCustom, calls=%fused_computation.2 | custom fusion | bytes 66048 | tf_op jit(solution)/shard_map/jit(diagonal)/gather | solution.py:111
  82.6 63.1 %copy.178 = f32[16,8,64,5,64]{2,4,3,1,0:T(8,128)} copy(f32[16,8,64,5,64]{0,1,4,2,3:T(8,128)} %bitcast.1) | data formatting | bytes 20971520 | tf_op jit(solution)/shard_map/transpose | solution.py:112
  146.0 2.3 copy.176
  148.3 1.7 reshape.238
  150.0 4.6 gather_fusion.2
  154.6 5.2 broadcast_select_fusion.1
  159.8 13.7 %reshape_reshape.7 = f32[16,8,320,32]{3,2,1,0:T(8,128)} reshape(f32[640,2048]{1,0:T(8,128)} %broadcast_select_fusion.1) | data formatting | bytes 10485760 | tf_op jit(solution)/shard_map/reshape;reshape | solution.py:123
  173.5 37.9 %bitcast_subtract_fusion.1 = f32[16,8,64,32]{2,3,1,0:T(8,128)S(1)} fusion(f32[16,8,64,32]{2,3,1,0:T(8,128)} %copy.182, f32[16,8,320,32]{3,2,1,0:T(8,128)} %reshape_reshape.7, f32[16,8,64,320]{2,3,1,0:T(8,128)} %bitcast.82, f32[16,8,64]{2,1,0:T(8,128)S(1)} %copy.181), kind=kOutput, calls=%fused_computation.13 | convolution fusion | flops 1007419392 | bytes 17858560 | tf_op jit(solution)/shard_map/ijor,ijrw->ijow/dot_general | solution.py:126
  211.7 1.9 collective-permute-start.4
  213.7 2.8 copy.184
  216.8 3.4 collective-permute-start.5
  220.2 3.6 reshape.242
  224.2 4.7 collective-permute-start.6
  228.9 1.9 collective-permute-start.7
  230.9 0.7 copy.196
  231.6 10.5 %all-to-all-start.1 = ((s32[128,1,2]{2,1,0:T(1,128)}), s32[128,1,2]{2,1,0:T(1,128)S(1)}, u32[]{:S(2)}, u32[]{:S(2)}) async-start(s32[128,1,2]{2,1,0:T(1,128)} %copy.196), calls=%async_computation.1 | async-start | bytes 131072 | tf_op jit(solution)/shard_map/all_to_all | solution.py:95
  242.2 1.8 pad_maximum_fusion
  244.0 1.7 reshape.243
  245.7 4.6 gather_fusion.3
  250.2 5.2 broadcast_select_fusion
  255.5 13.8 %reshape_reshape.8 = f32[16,8,320,32]{3,2,1,0:T(8,128)} reshape(f32[640,2048]{1,0:T(8,128)} %broadcast_select_fusion) | data formatting | bytes 10485760 | tf_op jit(solution)/shard_map/reshape;reshape | solution.py:123
  269.3 38.3 %multiply_reduce_fusion = (f32[32]{0:T(128)S(1)}, f32[16,8,64,32]{2,3,1,0:T(8,128)}) fusion(f32[16,8,64,32]{2,3,1,0:T(8,128)S(1)} %copy-done.1, f32[16,8,64]{2,1,0:T(8,128)S(1)} %copy.181, f32[16,8,320,32]{3,2,1,0:T(8,128)} %reshape_reshape.8, f32[16,8,64,320]{2,3,1,0:T(8,128)} %bitcast.83), kind=kOutput, calls=%fused_computation.14 | convolution fusion | flops 1007943680 | bytes 17858688 | tf_op jit(solution)/shard_map/ijor,ijrw->ijow/dot_general | solution.py:126
  307.6 65.2 %psum.7 = f32[32]{0:T(128)S(1)} all-reduce(f32[32]{0:T(128)S(1)} %get-tuple-element.33), channel_id=1, replica_groups=mesh['slab'=16,'pencil'=8] {'slab','pencil'}, use_global_device_ids=true, to_apply=%region_1.3 | all-reduce | flops 32 | bytes 256 | tf_op jit(solution)/shard_map/psum | solution.py:129
  372.8 2.0 broadcast_divide_fusion
  374.8 2.8 copy.188
  377.6 3.5 reshape_reshape_reshape.6
  381.2 1.1 fusion.7
  382.3 2.9 copy.192
  385.2 7.3 %all-to-all-start = ((f32[128,2,2048]{2,1,0:T(2,128)}), f32[128,2,2048]{2,1,0:T(2,128)S(1)}, u32[]{:S(2)}, u32[]{:S(2)}) async-start(f32[128,2,2048]{2,1,0:T(2,128)} %copy.192), calls=%async_computation | async-start | bytes 4194304 | tf_op jit(solution)/shard_map/all_to_all | solution.py:94
  393.1 0.8 reduce.13
  394.1 26.8 %all-to-all-done = f32[128,2,2048]{2,1,0:T(2,128)S(1)} async-done(((f32[128,2,2048]{2,1,0:T(2,128)}), f32[128,2,2048]{2,1,0:T(2,128)S(1)}, u32[]{:S(2)}, u32[]{:S(2)}) %all-to-all-start) | async-done | bytes 2097184 | tf_op jit(solution)/shard_map/all_to_all | solution.py:94
  421.0 5.3 reshape.246
  426.3 7.0 %copy.197 = f32[256,64,32]{0,1,2:T(8,128)S(1)} copy(f32[256,64,32]{2,1,0:T(8,128)} %reshape.246) | data formatting | bytes 4194304 | tf_op jit(solution)/shard_map/reshape | solution.py:148
  433.3 1.2 convolution_bitcast_fusion
  435.6 11.7 %custom-call.11 = f32[16,8,8]{2,1,0:T(8,128)S(1)} custom-call(f32[16,8,8]{2,1,0:T(8,128)S(1)} %fusion.18), custom_call_target="Cholesky" | custom-call | tf_op jit(solution)/shard_map/jit(cholesky)/cholesky | solution.py:44
  447.6 10.0 %custom-call.12 = f32[16,1,8,8]{2,3,1,0:T(8,128)S(1)} custom-call(f32[16,1,8,8]{3,2,1,0:T(8,128)S(1)} %select_bitcast_fusion), custom_call_target="InvertDiagBlocksLowerTriangular" | custom-call | tf_op jit(solution)/shard_map/jit(_solve_triangular)/vmap()/triangular_solve | solution.py:46
  459.0 11.2 %fusion.56 = f32[256,64,8]{2,1,0:T(8,128)} fusion(f32[256,64,32]{2,1,0:T(8,128)} %reshape.246, f32[256,32,8]{1,2,0:T(8,128)S(1)} %copy.209), kind=kOutput, calls=%fused_computation.114 | convolution fusion | flops 50331648 | bytes 2883584 | tf_op jit(solution)/shard_map/scv,svk->sck/dot_general | solution.py:153
  470.2 7.4 %reshape.249 = f32[128,2,512]{2,1,0:T(2,128)} reshape(f32[256,64,8]{2,1,0:T(8,128)} %fusion.56) | data formatting | bytes 1048576 | tf_op jit(solution)/shard_map/reshape | solution.py:159
  477.6 6.3 all-to-all-start.2
  484.1 11.8 %all-to-all-done.2 = f32[128,2,512]{2,1,0:T(2,128)S(1)} async-done(((f32[128,2,512]{2,1,0:T(2,128)}), f32[128,2,512]{2,1,0:T(2,128)S(1)}, u32[]{:S(2)}, u32[]{:S(2)}) %all-to-all-start.2) | async-done | bytes 524320 | tf_op jit(solution)/shard_map/all_to_all | solution.py:101
  496.3 3.8 collective-permute-start.8
  500.2 1.9 collective-permute-start.9
  502.2 4.6 collective-permute-done.9
  506.8 3.1 collective-permute-start.10
  509.9 2.7 collective-permute-start.11
  512.7 55.6 %copy.214 = f32[16,8,5,64,64]{4,3,2,1,0:T(8,128)} copy(f32[16,8,5,64,64]{0,1,4,3,2:T(8,128)} %bitcast) | data formatting | bytes 20971520 | tf_op jit(solution)/shard_map/reshape | solution.py:110
  568.4 4.5 reshape.244
  573.1 2.2 gather_fusion.1
  575.2 13.6 %gather.15 = f32[16,8,5,64,8]{4,3,2,1,0:T(8,128)} reshape(f32[640,512]{1,0:T(8,128)S(1)} %gather_fusion.1) | data formatting | bytes 2621440 | tf_op jit(solution)/shard_map/jit(_take)/gather | solution.py:60
  588.8 37.9 %fusion.4 = f32[16,8,5,64,8]{3,4,2,1,0:T(8,128)S(1)} fusion(f32[16,8,5,64,64]{4,3,2,1,0:T(8,128)} %copy.214, f32[16,8,5,64,8]{4,3,2,1,0:T(8,128)} %gather.15, pred[16,8,5]{2,1,0:T(8,128)(4,1)S(1)} %copy.211), kind=kOutput, calls=%fused_computation.16 | convolution fusion | flops 251985920 | bytes 13107840 | tf_op jit(solution)/shard_map/ijkoc,ijkcw->ijkow/dot_general | solution.py:166
  626.7 6.0 copy.215
  632.7 6.8 %copy.216 = f32[16,8,2560]{2,1,0:T(8,128)} copy(f32[16,8,2560]{0,2,1:T(8,128)} %bitcast.84) | data formatting | bytes 2621440
  (96 shorter events, 6.9 us)
Async XLA Ops:
  1.6 61.6 %collective-permute-start.1 = (f32[1,8,2048]{2,0,1:T(1,128)S(1)}, f32[1,8,2048]{2,0,1:T(1,128)S(1)}, u32[]{:S(2)}, u32[]{:S(2)}) collective-permute-start(f32[1,8,2048]{2,0,1:T(1,128)S(1)} %copy.174), channel_id=1, source_target_pairs={{8,0},{16,8},{24,16},{32,24},{40,32},{48,40},{56,48},{64,56},{72,6... | collective-permute-start | bytes 196616 | tf_op jit(solution)/shard_map/ppermute | solution.py:26
  4.1 59.0 %collective-permute-start = (f32[1,8,2048]{2,0,1:T(1,128)S(1)}, f32[1,8,2048]{2,0,1:T(1,128)S(1)}, u32[]{:S(2)}, u32[]{:S(2)}) collective-permute-start(f32[1,8,2048]{2,0,1:T(1,128)S(1)} %copy.173), channel_id=1, source_target_pairs={{0,8},{8,16},{16,24},{24,32},{32,40},{40,48},{48,56},{56,64},{64,7... | collective-permute-start | bytes 196616 | tf_op jit(solution)/shard_map/ppermute | solution.py:24
  11.6 39.3 %copy-start.4 = (s32[16,8,5]{2,1,0:T(8,128)}, s32[16,8,5]{2,1,0:T(8,128)S(1)}, u32[]{:S(2)}) copy-start(s32[16,8,5]{2,1,0:T(8,128)S(1)} %copy.172) | copy-start | bytes 7684
  11.9 39.0 %copy-start.7 = (s32[64]{0:T(128)}, s32[64]{0:T(128)S(1)}, u32[]{:S(2)}) copy-start(s32[64]{0:T(128)S(1)} %and_select_fusion.1) | copy-start | bytes 772
  50.9 11.7 %copy-start.2 = (f32[16,8,2048]{2,1,0:T(8,128)S(1)}, f32[16,8,2048]{2,1,0:T(8,128)}, u32[]{:S(2)}) copy-start(f32[16,8,2048]{2,1,0:T(8,128)} %param.9) | copy-start | bytes 3145732
  63.2 82.5 %collective-permute-start.2 = (f32[18,1,2048]{2,0,1:T(8,128)S(1)}, f32[18,1,2048]{2,0,1:T(8,128)S(1)}, u32[]{:S(2)}, u32[]{:S(2)}) collective-permute-start(f32[18,1,2048]{2,0,1:T(8,128)S(1)} %get-tuple-element.25), channel_id=1, source_target_pairs={{0,1},{1,2},{2,3},{3,4},{4,5},{5,6},{6,7},{8,9},{9,10},{10,11},{11... | collective-permute-start | bytes 442376 | tf_op jit(solution)/shard_map/ppermute | solution.py:24
  67.6 78.2 %collective-permute-start.3 = (f32[18,1,2048]{2,0,1:T(8,128)S(1)}, f32[18,1,2048]{2,0,1:T(8,128)S(1)}, u32[]{:S(2)}, u32[]{:S(2)}) collective-permute-start(f32[18,1,2048]{2,0,1:T(8,128)S(1)} %get-tuple-element.26), channel_id=1, source_target_pairs={{1,0},{2,1},{3,2},{4,3},{5,4},{6,5},{7,6},{9,8},{10,9},{11,10},{12... | collective-permute-start | bytes 442376 | tf_op jit(solution)/shard_map/ppermute | solution.py:26
  211.4 5.2 copy-start
  211.7 12.2 %collective-permute-start.4 = (f32[1,8,2048]{2,1,0:T(8,128)S(1)}, f32[1,8,2048]{2,1,0:T(8,128)S(1)}, u32[]{:S(2)}, u32[]{:S(2)}) collective-permute-start(f32[1,8,2048]{2,1,0:T(8,128)S(1)} %slice.78), channel_id=1, source_target_pairs={{0,8},{8,16},{16,24},{24,32},{32,40},{40,48},{48,56},{56,64},{64,7... | collective-permute-start | bytes 196616 | tf_op jit(solution)/shard_map/ppermute | solution.py:24
  216.8 7.1 %collective-permute-start.5 = (f32[1,8,2048]{2,1,0:T(8,128)S(1)}, f32[1,8,2048]{2,1,0:T(8,128)S(1)}, u32[]{:S(2)}, u32[]{:S(2)}) collective-permute-start(f32[1,8,2048]{2,1,0:T(8,128)S(1)} %slice.80), channel_id=1, source_target_pairs={{8,0},{16,8},{24,16},{32,24},{40,32},{48,40},{56,48},{64,56},{72,6... | collective-permute-start | bytes 196616 | tf_op jit(solution)/shard_map/ppermute | solution.py:26
  224.2 18.0 %collective-permute-start.6 = (f32[18,1,2048]{2,1,0:T(1,128)S(1)}, f32[18,1,2048]{2,1,0:T(1,128)S(1)}, u32[]{:S(2)}, u32[]{:S(2)}) collective-permute-start(f32[18,1,2048]{2,1,0:T(1,128)S(1)} %get-tuple-element.23), channel_id=1, source_target_pairs={{0,1},{1,2},{2,3},{3,4},{4,5},{5,6},{6,7},{8,9},{9,10},{10,11},{11... | collective-permute-start | bytes 442376 | tf_op jit(solution)/shard_map/ppermute | solution.py:24
  228.9 13.2 %collective-permute-start.7 = (f32[18,1,2048]{2,1,0:T(1,128)S(1)}, f32[18,1,2048]{2,1,0:T(1,128)S(1)}, u32[]{:S(2)}, u32[]{:S(2)}) collective-permute-start(f32[18,1,2048]{2,1,0:T(1,128)S(1)} %get-tuple-element.24), channel_id=1, source_target_pairs={{1,0},{2,1},{3,2},{4,3},{5,4},{6,5},{7,6},{9,8},{10,9},{11,10},{12... | collective-permute-start | bytes 442376 | tf_op jit(solution)/shard_map/ppermute | solution.py:26
  231.6 153.6 %all-to-all-start.1 = ((s32[128,1,2]{2,1,0:T(1,128)}), s32[128,1,2]{2,1,0:T(1,128)S(1)}, u32[]{:S(2)}, u32[]{:S(2)}) async-start(s32[128,1,2]{2,1,0:T(1,128)} %copy.196), calls=%async_computation.1 | async-start | bytes 131072 | tf_op jit(solution)/shard_map/all_to_all | solution.py:95
  255.5 13.8 %copy-start.1 = (f32[16,8,64,32]{2,3,1,0:T(8,128)S(1)}, f32[16,8,64,32]{2,3,1,0:T(8,128)}, u32[]{:S(2)}) copy-start(f32[16,8,64,32]{2,3,1,0:T(8,128)} %copy-done) | copy-start | bytes 3145732
  377.6 3.5 copy-start.8
  385.2 35.8 %all-to-all-start = ((f32[128,2,2048]{2,1,0:T(2,128)}), f32[128,2,2048]{2,1,0:T(2,128)S(1)}, u32[]{:S(2)}, u32[]{:S(2)}) async-start(f32[128,2,2048]{2,1,0:T(2,128)} %copy.192), calls=%async_computation | async-start | bytes 4194304 | tf_op jit(solution)/shard_map/all_to_all | solution.py:94
  470.2 13.7 %copy-start.5 = (s32[16,8,5]{2,1,0:T(8,128)S(1)}, s32[16,8,5]{2,1,0:T(8,128)}, u32[]{:S(2)}) copy-start(s32[16,8,5]{2,1,0:T(8,128)} %copy-done.4) | copy-start | bytes 7684
  477.6 18.3 %all-to-all-start.2 = ((f32[128,2,512]{2,1,0:T(2,128)}), f32[128,2,512]{2,1,0:T(2,128)S(1)}, u32[]{:S(2)}, u32[]{:S(2)}) async-start(f32[128,2,512]{2,1,0:T(2,128)} %reshape.249), calls=%async_computation.2 | async-start | bytes 1048576 | tf_op jit(solution)/shard_map/all_to_all | solution.py:101
  496.3 5.8 collective-permute-start.8
  500.1 68.1 %copy-start.3 = (f32[16,8,512]{2,1,0:T(8,128)}, f32[16,8,512]{2,1,0:T(8,128)S(1)}, u32[]{:S(2)}) copy-start(f32[16,8,512]{2,1,0:T(8,128)S(1)} %reshape_reshape_reshape.7) | copy-start | bytes 786436
  500.2 6.6 %collective-permute-start.9 = (f32[1,8,512]{2,1,0:T(8,128)S(1)}, f32[1,8,512]{2,1,0:T(8,128)S(1)}, u32[]{:S(2)}, u32[]{:S(2)}) collective-permute-start(f32[1,8,512]{2,1,0:T(8,128)S(1)} %slice.87), channel_id=1, source_target_pairs={{8,0},{16,8},{24,16},{32,24},{40,32},{48,40},{56,48},{64,56},{72,6... | collective-permute-start | bytes 49160 | tf_op jit(solution)/shard_map/ppermute | solution.py:26
  506.8 66.1 %collective-permute-start.10 = (f32[18,1,512]{2,1,0:T(1,128)S(1)}, f32[18,1,512]{2,1,0:T(1,128)S(1)}, u32[]{:S(2)}, u32[]{:S(2)}) collective-permute-start(f32[18,1,512]{2,1,0:T(1,128)S(1)} %get-tuple-element.29), channel_id=1, source_target_pairs={{0,1},{1,2},{2,3},{3,4},{4,5},{5,6},{6,7},{8,9},{9,10},{10,11},{11... | collective-permute-start | bytes 110600 | tf_op jit(solution)/shard_map/ppermute | solution.py:24
  509.9 63.0 %collective-permute-start.11 = (f32[18,1,512]{2,1,0:T(1,128)S(1)}, f32[18,1,512]{2,1,0:T(1,128)S(1)}, u32[]{:S(2)}, u32[]{:S(2)}) collective-permute-start(f32[18,1,512]{2,1,0:T(1,128)S(1)} %get-tuple-element.30), channel_id=1, source_target_pairs={{1,0},{2,1},{3,2},{4,3},{5,4},{6,5},{7,6},{9,8},{10,9},{11,10},{12... | collective-permute-start | bytes 110600 | tf_op jit(solution)/shard_map/ppermute | solution.py:26
  512.7 55.6 %copy-start.6 = (pred[16,8,5]{0,1,2:T(8,128)(4,1)S(1)}, pred[16,8,5]{0,1,2:T(8,128)(4,1)}, u32[]{:S(2)}) copy-start(pred[16,8,5]{0,1,2:T(8,128)(4,1)} %get-tuple-element.19) | copy-start | bytes 1924
where the time goes:
time: 651 us; the launch traced here: 640 us
  local copies, waits for them, and re-layouts  300 us (46%)
  matrix products  130 us (20%)
  blocking collectives  65.2 us (10%)
  starting transfers between devices  61.2 us (9%)
  waiting for transfers between devices  43.2 us (7%)
  other arithmetic  39.2 us (6%)
    dot_general x2, matrix products, shards(): jnp.einsum('ijor,ijrw->ijow', block_wide, picked, precision=FULL_PRECISION)  76.2 us
    psum x1, blocking collectives, shards(): totals = lax.psum(squares, ('slab', 'pencil'))  65.2 us
    transpose x1, local copies, waits for them, and re-layouts, shards(): jnp.transpose(blocks, (0, 1, 3, 2, 4))  63.1 us
    reshape x1, local copies, waits for them, and re-layouts, shards(): blocks = a_blocks.reshape(height, across_devices, KS, BLK, BLK)  55.6 us
    unnamed x27, local copies, waits for them, and re-layouts  47.3 us
    dot_general x1, matrix products, shards(): jnp.einsum('ijkoc,ijkcw->ijkow', blocks, picked_tiles, precision=FULL_PRE...  37.9 us
    another operation x2, local copies, waits for them, and re-layouts, shards(): pick_rows(padded, flat_index, height, across_devices)  27.5 us
    all_to_all x1, waiting for transfers between devices, send_owner(): lax.all_to_all(payload, ('slab', 'pencil'), split_axis=0, concat_axis=0,...  26.8 us
  transfers between devices with their start and end apart: 15, of which 3 were waited for; matrix products, arithmetic and copies ran while one was open for 43% of the time, Pallas kernels for 0%

commit v1 on v0

--- a/solution.py
+++ b/solution.py
@@ -126,7 +126,7 @@
         image = jnp.einsum("ijor,ijrw->ijow", block_wide, picked, precision=FULL_PRECISION)
         candidate_vectors = candidate_vectors - OMEGA * image / diagonal[:, :, :, None]
     squares = jnp.sum(candidate_vectors * candidate_vectors, axis=(0, 1, 2))
-    totals = lax.psum(squares, ("slab", "pencil"))
+    totals = lax.psum(lax.psum(squares, "pencil"), "slab")
     scale = jnp.sqrt(totals / (height * across_devices * BLK * devices) + 1e-06)
     relaxed = candidate_vectors / scale
     block_rows = height * across_devices

time: 651 us -> 639 us (0.982)
  blocking collectives: 65.2 us -> 38 us
  starting transfers between devices: 61.2 us -> 76.4 us
    psum x1 -> x2, blocking collectives: 65.2 us -> 38 us  [shards(): totals = lax.psum(lax.psum(squares, 'pencil'), 'slab')]
    all_to_all x1, starting transfers between devices: 7.26 us -> 22.3 us  [send_owner(): lax.all_to_all(payload, ('slab', 'pencil'), split_axis=0, concat_axis=0,...]
  transfers between devices with their start and end apart: 15 -> 15, of which waited for: 3 -> 3; matrix products, arithmetic and copies ran while one was open for 43% -> 44% of each run, Pallas kernels for 0% -> 0%
where the time goes in v1:
time: 639 us; the launch traced here: 628 us
  local copies, waits for them, and re-layouts  300 us (47%)
  matrix products  129 us (20%)
  starting transfers between devices  76.4 us (12%)
  waiting for transfers between devices  43.3 us (7%)
  other arithmetic  39.3 us (6%)
  blocking collectives  38 us (6%)
    dot_general x2, matrix products, shards(): jnp.einsum('ijor,ijrw->ijow', block_wide, picked, precision=FULL_PRECISION)  75.9 us
    transpose x1, local copies, waits for them, and re-layouts, shards(): jnp.transpose(blocks, (0, 1, 3, 2, 4))  63.1 us
    reshape x1, local copies, waits for them, and re-layouts, shards(): blocks = a_blocks.reshape(height, across_devices, KS, BLK, BLK)  55.7 us
    unnamed x27, local copies, waits for them, and re-layouts  47.3 us
    psum x2, blocking collectives, shards(): totals = lax.psum(lax.psum(squares, 'pencil'), 'slab')  38 us
    dot_general x1, matrix products, shards(): jnp.einsum('ijkoc,ijkcw->ijkow', blocks, picked_tiles, precision=FULL_PRE...  37.9 us
    another operation x2, local copies, waits for them, and re-layouts, shards(): pick_rows(padded, flat_index, height, across_devices)  27.5 us
    all_to_all x1, waiting for transfers between devices, send_owner(): lax.all_to_all(payload, ('slab', 'pencil'), split_axis=0, concat_axis=0,...  26.9 us
  transfers between devices with their start and end apart: 15, of which 3 were waited for; matrix products, arithmetic and copies ran while one was open for 44% of the time, Pallas kernels for 0%

profile of v1, /device:TPU:7, one launch (start us, length us, event | category | flops | bytes accessed | tf_op | source)
XLA Modules:
  0.0 627.7 jit_solution(1579738094764714344)
XLA Ops:
  0.6 0.9 fusion.53
  1.6 2.5 collective-permute-start.1
  4.1 4.9 collective-permute-start
  9.1 0.8 copy.189
  10.1 1.4 compare_and_fusion
  11.9 38.9 %copy.177 = f32[16,8,20480]{0,1,2:T(8,128)} copy(f32[16,8,20480]{2,1,0:T(8,128)} %param.6) | data formatting | bytes 20971520 | tf_op args[0]
  50.9 11.6 %slice_bitcast_fusion = f32[16,8,64,64]{0,1,3,2:T(8,128)} fusion(f32[16,8,5,64,64]{0,1,4,3,2:T(8,128)} %bitcast), kind=kLoop, calls=%fused_computation.6 | loop fusion | bytes 4194304 | tf_op jit(solution)/shard_map/squeeze | solution.py:111
  63.2 4.3 collective-permute-start.2
  67.6 1.9 collective-permute-start.3
  69.5 2.7 reshape.237
  72.2 3.8 copy.182
  76.0 6.4 %gather_fusion = f32[64,16,8]{1,2,0:T(8,128)S(1)} fusion(f32[16,8,64,64]{0,1,3,2:T(8,128)} %slice_bitcast_fusion, s32[64]{0:T(128)S(1)} %or_bitcast_fusion), kind=kCustom, calls=%fused_computation.2 | custom fusion | bytes 66048 | tf_op jit(solution)/shard_map/jit(diagonal)/gather | solution.py:111
  82.6 63.1 %copy.178 = f32[16,8,64,5,64]{2,4,3,1,0:T(8,128)} copy(f32[16,8,64,5,64]{0,1,4,2,3:T(8,128)} %bitcast.1) | data formatting | bytes 20971520 | tf_op jit(solution)/shard_map/transpose | solution.py:112
  146.1 2.3 copy.176
  148.3 1.7 reshape.238
  150.0 4.6 gather_fusion.2
  154.6 5.2 broadcast_select_fusion.1
  159.8 13.7 %reshape_reshape.7 = f32[16,8,320,32]{3,2,1,0:T(8,128)} reshape(f32[640,2048]{1,0:T(8,128)} %broadcast_select_fusion.1) | data formatting | bytes 10485760 | tf_op jit(solution)/shard_map/reshape;reshape | solution.py:123
  173.5 37.6 %bitcast_subtract_fusion.1 = f32[16,8,64,32]{2,3,1,0:T(8,128)S(1)} fusion(f32[16,8,64,32]{2,3,1,0:T(8,128)} %copy.182, f32[16,8,320,32]{3,2,1,0:T(8,128)} %reshape_reshape.7, f32[16,8,64,320]{2,3,1,0:T(8,128)} %bitcast.82, f32[16,8,64]{2,1,0:T(8,128)S(1)} %copy.181), kind=kOutput, calls=%fused_computation.13 | convolution fusion | flops 1007419392 | bytes 17858560 | tf_op jit(solution)/shard_map/ijor,ijrw->ijow/dot_general | solution.py:126
  211.4 1.9 collective-permute-start.4
  213.4 2.8 copy.184
  216.5 3.4 collective-permute-start.5
  219.9 3.6 reshape.242
  223.9 4.7 collective-permute-start.6
  228.6 1.9 collective-permute-start.7
  230.6 0.7 copy.196
  231.3 10.8 %all-to-all-start.1 = ((s32[128,1,2]{2,1,0:T(1,128)}), s32[128,1,2]{2,1,0:T(1,128)S(1)}, u32[]{:S(2)}, u32[]{:S(2)}) async-start(s32[128,1,2]{2,1,0:T(1,128)} %copy.196), calls=%async_computation.1 | async-start | bytes 131072 | tf_op jit(solution)/shard_map/all_to_all | solution.py:95
  242.1 1.8 pad_maximum_fusion
  243.9 1.7 reshape.243
  245.6 4.6 gather_fusion.3
  250.2 5.2 broadcast_select_fusion
  255.4 13.8 %reshape_reshape.8 = f32[16,8,320,32]{3,2,1,0:T(8,128)} reshape(f32[640,2048]{1,0:T(8,128)} %broadcast_select_fusion) | data formatting | bytes 10485760 | tf_op jit(solution)/shard_map/reshape;reshape | solution.py:123
  269.2 38.3 %multiply_reduce_fusion = (f32[32]{0:T(128)S(1)}, f32[16,8,64,32]{2,3,1,0:T(8,128)}) fusion(f32[16,8,64,32]{2,3,1,0:T(8,128)S(1)} %copy-done.1, f32[16,8,64]{2,1,0:T(8,128)S(1)} %copy.181, f32[16,8,320,32]{3,2,1,0:T(8,128)} %reshape_reshape.8, f32[16,8,64,320]{2,3,1,0:T(8,128)} %bitcast.83), kind=kOutput, calls=%fused_computation.14 | convolution fusion | flops 1007943680 | bytes 17858688 | tf_op jit(solution)/shard_map/ijor,ijrw->ijow/dot_general | solution.py:126
  307.5 12.1 %psum.14 = f32[32]{0:T(128)S(1)} all-reduce(f32[32]{0:T(128)S(1)} %get-tuple-element.33), channel_id=1, replica_groups=mesh['slab'=16,'pencil'=8] {'pencil'}, use_global_device_ids=true, to_apply=%region_1.3 | all-reduce | flops 32 | bytes 256 | tf_op jit(solution)/shard_map/psum | solution.py:129
  319.6 25.9 %psum.15 = f32[32]{0:T(128)S(1)} all-reduce(f32[32]{0:T(128)S(1)} %psum.14), channel_id=1, replica_groups=mesh['slab'=16,'pencil'=8] {'slab'}, use_global_device_ids=true, to_apply=%region_2.4 | all-reduce | flops 32 | bytes 256 | tf_op jit(solution)/shard_map/psum | solution.py:129
  345.5 2.0 broadcast_divide_fusion
  347.5 2.8 copy.188
  350.4 3.5 reshape_reshape_reshape.6
  353.9 1.1 fusion.7
  355.0 2.9 copy.192
  358.0 22.3 %all-to-all-start = ((f32[128,2,2048]{2,1,0:T(2,128)}), f32[128,2,2048]{2,1,0:T(2,128)S(1)}, u32[]{:S(2)}, u32[]{:S(2)}) async-start(f32[128,2,2048]{2,1,0:T(2,128)} %copy.192), calls=%async_computation | async-start | bytes 4194304 | tf_op jit(solution)/shard_map/all_to_all | solution.py:94
  380.8 0.8 reduce.13
  381.9 26.9 %all-to-all-done = f32[128,2,2048]{2,1,0:T(2,128)S(1)} async-done(((f32[128,2,2048]{2,1,0:T(2,128)}), f32[128,2,2048]{2,1,0:T(2,128)S(1)}, u32[]{:S(2)}, u32[]{:S(2)}) %all-to-all-start) | async-done | bytes 2097184 | tf_op jit(solution)/shard_map/all_to_all | solution.py:94
  408.9 5.3 reshape.246
  414.2 7.0 %copy.197 = f32[256,64,32]{0,1,2:T(8,128)S(1)} copy(f32[256,64,32]{2,1,0:T(8,128)} %reshape.246) | data formatting | bytes 4194304 | tf_op jit(solution)/shard_map/reshape | solution.py:148
  421.2 1.2 convolution_bitcast_fusion
  423.5 11.7 %custom-call.11 = f32[16,8,8]{2,1,0:T(8,128)S(1)} custom-call(f32[16,8,8]{2,1,0:T(8,128)S(1)} %fusion.18), custom_call_target="Cholesky" | custom-call | tf_op jit(solution)/shard_map/jit(cholesky)/cholesky | solution.py:44
  435.4 10.0 %custom-call.12 = f32[16,1,8,8]{2,3,1,0:T(8,128)S(1)} custom-call(f32[16,1,8,8]{3,2,1,0:T(8,128)S(1)} %select_bitcast_fusion), custom_call_target="InvertDiagBlocksLowerTriangular" | custom-call | tf_op jit(solution)/shard_map/jit(_solve_triangular)/vmap()/triangular_solve | solution.py:46
  446.9 11.2 %fusion.56 = f32[256,64,8]{2,1,0:T(8,128)} fusion(f32[256,64,32]{2,1,0:T(8,128)} %reshape.246, f32[256,32,8]{1,2,0:T(8,128)S(1)} %copy.209), kind=kOutput, calls=%fused_computation.114 | convolution fusion | flops 50331648 | bytes 2883584 | tf_op jit(solution)/shard_map/scv,svk->sck/dot_general | solution.py:153
  458.0 7.4 %reshape.249 = f32[128,2,512]{2,1,0:T(2,128)} reshape(f32[256,64,8]{2,1,0:T(8,128)} %fusion.56) | data formatting | bytes 1048576 | tf_op jit(solution)/shard_map/reshape | solution.py:159
  465.4 6.3 %all-to-all-start.2 = ((f32[128,2,512]{2,1,0:T(2,128)}), f32[128,2,512]{2,1,0:T(2,128)S(1)}, u32[]{:S(2)}, u32[]{:S(2)}) async-start(f32[128,2,512]{2,1,0:T(2,128)} %reshape.249), calls=%async_computation.2 | async-start | bytes 1048576 | tf_op jit(solution)/shard_map/all_to_all | solution.py:101
  471.9 11.8 %all-to-all-done.2 = f32[128,2,512]{2,1,0:T(2,128)S(1)} async-done(((f32[128,2,512]{2,1,0:T(2,128)}), f32[128,2,512]{2,1,0:T(2,128)S(1)}, u32[]{:S(2)}, u32[]{:S(2)}) %all-to-all-start.2) | async-done | bytes 524320 | tf_op jit(solution)/shard_map/all_to_all | solution.py:101
  484.2 3.8 collective-permute-start.8
  488.0 1.9 collective-permute-start.9
  490.0 4.6 collective-permute-done.9
  494.7 3.1 collective-permute-start.10
  497.8 2.7 collective-permute-start.11
  500.5 55.7 %copy.214 = f32[16,8,5,64,64]{4,3,2,1,0:T(8,128)} copy(f32[16,8,5,64,64]{0,1,4,3,2:T(8,128)} %bitcast) | data formatting | bytes 20971520 | tf_op jit(solution)/shard_map/reshape | solution.py:110
  556.3 4.5 reshape.244
  561.0 2.2 gather_fusion.1
  563.2 13.5 %gather.15 = f32[16,8,5,64,8]{4,3,2,1,0:T(8,128)} reshape(f32[640,512]{1,0:T(8,128)S(1)} %gather_fusion.1) | data formatting | bytes 2621440 | tf_op jit(solution)/shard_map/jit(_take)/gather | solution.py:60
  576.7 37.9 %fusion.4 = f32[16,8,5,64,8]{3,4,2,1,0:T(8,128)S(1)} fusion(f32[16,8,5,64,64]{4,3,2,1,0:T(8,128)} %copy.214, f32[16,8,5,64,8]{4,3,2,1,0:T(8,128)} %gather.15, pred[16,8,5]{2,1,0:T(8,128)(4,1)S(1)} %copy.211), kind=kOutput, calls=%fused_computation.16 | convolution fusion | flops 251985920 | bytes 13107840 | tf_op jit(solution)/shard_map/ijkoc,ijkcw->ijkow/dot_general | solution.py:166
  614.6 6.1 copy.215
  620.7 6.8 %copy.216 = f32[16,8,2560]{2,1,0:T(8,128)} copy(f32[16,8,2560]{0,2,1:T(8,128)} %bitcast.84) | data formatting | bytes 2621440
  (97 shorter events, 7.5 us)
Async XLA Ops:
  1.6 61.6 %collective-permute-start.1 = (f32[1,8,2048]{2,0,1:T(1,128)S(1)}, f32[1,8,2048]{2,0,1:T(1,128)S(1)}, u32[]{:S(2)}, u32[]{:S(2)}) collective-permute-start(f32[1,8,2048]{2,0,1:T(1,128)S(1)} %copy.174), channel_id=1, source_target_pairs={{8,0},{16,8},{24,16},{32,24},{40,32},{48,40},{56,48},{64,56},{72,6... | collective-permute-start | bytes 196616 | tf_op jit(solution)/shard_map/ppermute | solution.py:26
  4.1 59.0 %collective-permute-start = (f32[1,8,2048]{2,0,1:T(1,128)S(1)}, f32[1,8,2048]{2,0,1:T(1,128)S(1)}, u32[]{:S(2)}, u32[]{:S(2)}) collective-permute-start(f32[1,8,2048]{2,0,1:T(1,128)S(1)} %copy.173), channel_id=1, source_target_pairs={{0,8},{8,16},{16,24},{24,32},{32,40},{40,48},{48,56},{56,64},{64,7... | collective-permute-start | bytes 196616 | tf_op jit(solution)/shard_map/ppermute | solution.py:24
  11.6 39.3 %copy-start.4 = (s32[16,8,5]{2,1,0:T(8,128)}, s32[16,8,5]{2,1,0:T(8,128)S(1)}, u32[]{:S(2)}) copy-start(s32[16,8,5]{2,1,0:T(8,128)S(1)} %copy.172) | copy-start | bytes 7684
  11.9 39.0 %copy-start.7 = (s32[64]{0:T(128)}, s32[64]{0:T(128)S(1)}, u32[]{:S(2)}) copy-start(s32[64]{0:T(128)S(1)} %and_select_fusion.1) | copy-start | bytes 772
  50.9 11.7 %copy-start.2 = (f32[16,8,2048]{2,1,0:T(8,128)S(1)}, f32[16,8,2048]{2,1,0:T(8,128)}, u32[]{:S(2)}) copy-start(f32[16,8,2048]{2,1,0:T(8,128)} %param.9) | copy-start | bytes 3145732
  63.2 82.5 %collective-permute-start.2 = (f32[18,1,2048]{2,0,1:T(8,128)S(1)}, f32[18,1,2048]{2,0,1:T(8,128)S(1)}, u32[]{:S(2)}, u32[]{:S(2)}) collective-permute-start(f32[18,1,2048]{2,0,1:T(8,128)S(1)} %get-tuple-element.25), channel_id=1, source_target_pairs={{0,1},{1,2},{2,3},{3,4},{4,5},{5,6},{6,7},{8,9},{9,10},{10,11},{11... | collective-permute-start | bytes 442376 | tf_op jit(solution)/shard_map/ppermute | solution.py:24
  67.6 78.2 %collective-permute-start.3 = (f32[18,1,2048]{2,0,1:T(8,128)S(1)}, f32[18,1,2048]{2,0,1:T(8,128)S(1)}, u32[]{:S(2)}, u32[]{:S(2)}) collective-permute-start(f32[18,1,2048]{2,0,1:T(8,128)S(1)} %get-tuple-element.26), channel_id=1, source_target_pairs={{1,0},{2,1},{3,2},{4,3},{5,4},{6,5},{7,6},{9,8},{10,9},{11,10},{12... | collective-permute-start | bytes 442376 | tf_op jit(solution)/shard_map/ppermute | solution.py:26
  211.1 5.2 copy-start
  211.4 12.2 %collective-permute-start.4 = (f32[1,8,2048]{2,1,0:T(8,128)S(1)}, f32[1,8,2048]{2,1,0:T(8,128)S(1)}, u32[]{:S(2)}, u32[]{:S(2)}) collective-permute-start(f32[1,8,2048]{2,1,0:T(8,128)S(1)} %slice.78), channel_id=1, source_target_pairs={{0,8},{8,16},{16,24},{24,32},{32,40},{40,48},{48,56},{56,64},{64,7... | collective-permute-start | bytes 196616 | tf_op jit(solution)/shard_map/ppermute | solution.py:24
  216.5 7.1 %collective-permute-start.5 = (f32[1,8,2048]{2,1,0:T(8,128)S(1)}, f32[1,8,2048]{2,1,0:T(8,128)S(1)}, u32[]{:S(2)}, u32[]{:S(2)}) collective-permute-start(f32[1,8,2048]{2,1,0:T(8,128)S(1)} %slice.80), channel_id=1, source_target_pairs={{8,0},{16,8},{24,16},{32,24},{40,32},{48,40},{56,48},{64,56},{72,6... | collective-permute-start | bytes 196616 | tf_op jit(solution)/shard_map/ppermute | solution.py:26
  223.9 18.2 %collective-permute-start.6 = (f32[18,1,2048]{2,1,0:T(1,128)S(1)}, f32[18,1,2048]{2,1,0:T(1,128)S(1)}, u32[]{:S(2)}, u32[]{:S(2)}) collective-permute-start(f32[18,1,2048]{2,1,0:T(1,128)S(1)} %get-tuple-element.23), channel_id=1, source_target_pairs={{0,1},{1,2},{2,3},{3,4},{4,5},{5,6},{6,7},{8,9},{9,10},{10,11},{11... | collective-permute-start | bytes 442376 | tf_op jit(solution)/shard_map/ppermute | solution.py:24
  228.6 13.5 %collective-permute-start.7 = (f32[18,1,2048]{2,1,0:T(1,128)S(1)}, f32[18,1,2048]{2,1,0:T(1,128)S(1)}, u32[]{:S(2)}, u32[]{:S(2)}) collective-permute-start(f32[18,1,2048]{2,1,0:T(1,128)S(1)} %get-tuple-element.24), channel_id=1, source_target_pairs={{1,0},{2,1},{3,2},{4,3},{5,4},{6,5},{7,6},{9,8},{10,9},{11,10},{12... | collective-permute-start | bytes 442376 | tf_op jit(solution)/shard_map/ppermute | solution.py:26
  231.3 126.6 %all-to-all-start.1 = ((s32[128,1,2]{2,1,0:T(1,128)}), s32[128,1,2]{2,1,0:T(1,128)S(1)}, u32[]{:S(2)}, u32[]{:S(2)}) async-start(s32[128,1,2]{2,1,0:T(1,128)} %copy.196), calls=%async_computation.1 | async-start | bytes 131072 | tf_op jit(solution)/shard_map/all_to_all | solution.py:95
  255.4 13.8 %copy-start.1 = (f32[16,8,64,32]{2,3,1,0:T(8,128)S(1)}, f32[16,8,64,32]{2,3,1,0:T(8,128)}, u32[]{:S(2)}) copy-start(f32[16,8,64,32]{2,3,1,0:T(8,128)} %copy-done) | copy-start | bytes 3145732
  350.4 3.5 copy-start.8
  358.0 50.9 %all-to-all-start = ((f32[128,2,2048]{2,1,0:T(2,128)}), f32[128,2,2048]{2,1,0:T(2,128)S(1)}, u32[]{:S(2)}, u32[]{:S(2)}) async-start(f32[128,2,2048]{2,1,0:T(2,128)} %copy.192), calls=%async_computation | async-start | bytes 4194304 | tf_op jit(solution)/shard_map/all_to_all | solution.py:94
  458.0 13.7 %copy-start.5 = (s32[16,8,5]{2,1,0:T(8,128)S(1)}, s32[16,8,5]{2,1,0:T(8,128)}, u32[]{:S(2)}) copy-start(s32[16,8,5]{2,1,0:T(8,128)} %copy-done.4) | copy-start | bytes 7684
  465.4 18.3 %all-to-all-start.2 = ((f32[128,2,512]{2,1,0:T(2,128)}), f32[128,2,512]{2,1,0:T(2,128)S(1)}, u32[]{:S(2)}, u32[]{:S(2)}) async-start(f32[128,2,512]{2,1,0:T(2,128)} %reshape.249), calls=%async_computation.2 | async-start | bytes 1048576 | tf_op jit(solution)/shard_map/all_to_all | solution.py:101
  484.2 5.8 collective-permute-start.8
  488.0 68.2 %copy-start.3 = (f32[16,8,512]{2,1,0:T(8,128)}, f32[16,8,512]{2,1,0:T(8,128)S(1)}, u32[]{:S(2)}) copy-start(f32[16,8,512]{2,1,0:T(8,128)S(1)} %reshape_reshape_reshape.7) | copy-start | bytes 786436
  488.0 6.6 %collective-permute-start.9 = (f32[1,8,512]{2,1,0:T(8,128)S(1)}, f32[1,8,512]{2,1,0:T(8,128)S(1)}, u32[]{:S(2)}, u32[]{:S(2)}) collective-permute-start(f32[1,8,512]{2,1,0:T(8,128)S(1)} %slice.87), channel_id=1, source_target_pairs={{8,0},{16,8},{24,16},{32,24},{40,32},{48,40},{56,48},{64,56},{72,6... | collective-permute-start | bytes 49160 | tf_op jit(solution)/shard_map/ppermute | solution.py:26
  494.7 66.1 %collective-permute-start.10 = (f32[18,1,512]{2,1,0:T(1,128)S(1)}, f32[18,1,512]{2,1,0:T(1,128)S(1)}, u32[]{:S(2)}, u32[]{:S(2)}) collective-permute-start(f32[18,1,512]{2,1,0:T(1,128)S(1)} %get-tuple-element.29), channel_id=1, source_target_pairs={{0,1},{1,2},{2,3},{3,4},{4,5},{5,6},{6,7},{8,9},{9,10},{10,11},{11... | collective-permute-start | bytes 110600 | tf_op jit(solution)/shard_map/ppermute | solution.py:24
  497.8 63.0 %collective-permute-start.11 = (f32[18,1,512]{2,1,0:T(1,128)S(1)}, f32[18,1,512]{2,1,0:T(1,128)S(1)}, u32[]{:S(2)}, u32[]{:S(2)}) collective-permute-start(f32[18,1,512]{2,1,0:T(1,128)S(1)} %get-tuple-element.30), channel_id=1, source_target_pairs={{1,0},{2,1},{3,2},{4,3},{5,4},{6,5},{7,6},{9,8},{10,9},{11,10},{12... | collective-permute-start | bytes 110600 | tf_op jit(solution)/shard_map/ppermute | solution.py:26
  500.5 55.7 %copy-start.6 = (pred[16,8,5]{0,1,2:T(8,128)(4,1)S(1)}, pred[16,8,5]{0,1,2:T(8,128)(4,1)}, u32[]{:S(2)}) copy-start(pred[16,8,5]{0,1,2:T(8,128)(4,1)} %get-tuple-element.19) | copy-start | bytes 1924
